TPU v7x, 32 devices: a whole 2x2x4 slice. The times are simulated.
32 devices in a mesh: dp: 8 (over y, x, core), tensor: 4 (over z).
Axes of the slice: x: 2, y: 2, z: 4, core: 2. Of those that a mesh axis runs over, the one named last changes fastest.
Arguments:
- activations: bfloat16 [4096, 8192], P('dp', 'tensor'), may hold values from -6 to 6
- out_grads: bfloat16 [4096, 28672], P('dp', 'tensor'), may hold values from -6 to 6
- input_proj: bfloat16 [8192, 64], P('tensor'), may hold values from -0.0625 to 0.0625
- grad_proj: bfloat16 [28672, 64], P('tensor'), may hold values from -4 to 4, as said below
- example_count: int32 [8], P('dp'), may hold values from 1 to 4, as said below
- child_order: int32 [8], replicated, may hold values 0 or 1
- prior_sketch: float32 [2048, 4096], P('dp', 'tensor'), may hold values from -6 to 6
- fold_map: float32 [256, 4], replicated, may hold values from -3 to 3
- merge_mix: float32 [256, 512], replicated, may hold values from -0.25 to 0.25
Outputs:
- merged_sketch: float32 [256, 4096], P(None, 'tensor')
- preconditioned: float32 [32, 4096], P('dp', 'tensor')
Inputs may be any that keep to these rules, and one draw needn't show every extreme that they name: `example_count`: some data rank has exactly 4 live examples. `grad_proj`: entries within 26 / sqrt(28672) of zero.
All inputs are finite; a program needn't handle non-finite values.
Results may differ from a plain program's by a relative error of at most 0.0003.
Values sent between devices are 32-bit elements; how exact they have to be, the bound alone decides.
A program may use at most 64 MiB of HBM per device.

v0:
```python
import jax
import jax.numpy as jnp
from jax import lax
from jax.sharding import PartitionSpec as P

RANK = 64
SEQ = 128


def from_partner(value, axis, stride):
    mask = 2**stride
    pairs = [(source, source ^ mask) for source in range(lax.axis_size(axis))]
    return lax.ppermute(value, axis, pairs)


def body(
    activations,
    out_grads,
    input_proj,
    grad_proj,
    example_count,
    child_order,
    prior_sketch,
    fold_map,
    merge_mix,
):
    tensor_count = lax.axis_size("tensor")
    own_rank = RANK // tensor_count
    example_slots = activations.shape[0] // SEQ
    sketch_rows = prior_sketch.shape[0]
    input_part = jnp.dot(activations, input_proj, preferred_element_type=jnp.float32)
    grad_part = jnp.dot(out_grads, grad_proj, preferred_element_type=jnp.float32)
    input_side, grad_side = lax.psum((input_part, grad_part), "tensor")
    grad_own = lax.dynamic_slice_in_dim(grad_side, lax.axis_index("tensor") * own_rank, own_rank, 1)
    grad_blocks = grad_own.reshape(example_slots, SEQ, own_rank)
    input_blocks = input_side.reshape(example_slots, SEQ, RANK)
    example_grad = jnp.einsum(
        "eta,etb->eab", grad_blocks, input_blocks, precision=lax.Precision.HIGHEST
    )
    example_grad = example_grad.reshape(example_slots, own_rank * RANK) / jnp.sqrt(jnp.float32(SEQ))
    live = jnp.arange(example_slots, dtype=jnp.int32) < example_count[0]
    example_grad = jnp.where(live[:, None], example_grad, jnp.zeros_like(example_grad))
    leaf_node = prior_sketch + jnp.dot(fold_map, example_grad, precision=lax.Precision.HIGHEST)
    leaf_weight = lax.psum(jnp.sum(leaf_node * leaf_node), "tensor")
    mix_first = merge_mix[:, :sketch_rows]
    mix_second = merge_mix[:, sketch_rows:]
    depth_count = lax.axis_size("dp").bit_length() - 1
    rank_index = lax.axis_index("dp")
    sketch_node = leaf_node
    sketch_weight = leaf_weight
    for level_index in range(depth_count):
        sibling_node, sibling_weight = from_partner((sketch_node, sketch_weight), "dp", level_index)
        upper_half = rank_index >> level_index & 1
        block_start = rank_index >> level_index + 1 << level_index + 1
        flip_order = child_order[block_start + (1 << level_index) - 1]
        own_first = upper_half == flip_order
        first = jnp.where(own_first, sketch_node, sibling_node)
        second = jnp.where(own_first, sibling_node, sketch_node)
        first_weight = jnp.where(own_first, sketch_weight, sibling_weight)
        second_weight = jnp.where(own_first, sibling_weight, sketch_weight)
        mixture = jnp.dot(mix_first, first, precision=lax.Precision.HIGHEST) + jnp.dot(
            mix_second, second, precision=lax.Precision.HIGHEST
        )
        mix_total = lax.psum(jnp.sum(mixture * mixture), "tensor")
        sketch_weight = first_weight + second_weight
        sketch_node = mixture * jnp.sqrt(sketch_weight / (mix_total + 1e-06))
    gram_part = jnp.dot(sketch_node, sketch_node.T, precision=lax.Precision.HIGHEST)
    product_part = jnp.dot(sketch_node, example_grad.T, precision=lax.Precision.HIGHEST)
    gram, sketch_grad = lax.psum((gram_part, product_part), "tensor")
    damping = jnp.trace(gram) / sketch_rows
    system = gram + damping * jnp.eye(sketch_rows, dtype=jnp.float32)
    factor = jnp.linalg.cholesky(system)
    solved = jax.scipy.linalg.cho_solve((factor, True), sketch_grad)
    preconditioned = example_grad - jnp.dot(solved.T, sketch_node, precision=lax.Precision.HIGHEST)
    return (sketch_node, preconditioned)


def solution(mesh):
    in_specs = (
        P("dp", "tensor"),
        P("dp", "tensor"),
        P("tensor", None),
        P("tensor", None),
        P("dp"),
        P(),
        P("dp", "tensor"),
        P(),
        P(),
    )
    out_specs = (P(None, "tensor"), P("dp", "tensor"))
    return jax.shard_map(body, mesh=mesh, in_specs=in_specs, out_specs=out_specs, check_vma=False)
```

profile of v0, /device:TPU:0, one launch (start us, length us, event | category | flops | bytes accessed | tf_op | source)
XLA Modules:
  0.0 291.9 jit_solution(15050861464168036459)
XLA Ops:
  7.2 1.5 copy-done
  8.8 1.7 convolution_bitcast_fusion.1
  11.1 6.3 %fusion.57 = f32[512,64]{0,1:T(8,128)} fusion(bf16[512,7168]{1,0:T(8,128)(2,1)} %param.10, bf16[7168,64]{0,1:T(8,128)(2,1)} %param.12), kind=kOutput, calls=%fused_computation.97 | convolution fusion | flops 469762048 | bytes 8388608 | tf_op jit(solution)/shard_map/dot_general | solution.py:32
  18.1 1.3 copy.22
  19.5 36.5 %all-reduce.8.cloned.1.call-done = (f32[4,128,64]{1,2,0:T(8,128)}, f32[512,64]{0,1:T(8,128)}) async-done(((f32[4,128,64]{1,2,0:T(8,128)}, f32[512,64]{0,1:T(8,128)}), (f32[4,128,64]{1,2,0:T(8,128)}, f32[512,64]{0,1:T(8,128)})) %all-reduce.8.cloned.1.call-update) | async-done | bytes 262160 | tf_op jit(solution)/shard_map/psum | solution.py:33
  56.0 1.2 convolution_multiply_fusion
  57.3 2.9 %multiply_reduce_fusion.3 = (f32[]{:T(128)}, f32[256,1024]{0,1:T(8,128)S(1)}) fusion(f32[256,1024]{0,1:T(8,128)} %copy.22, f32[256,4]{0,1:T(4,128)S(1)} %copy-done.5, f32[4,1024]{1,0:T(4,128)S(1)} %div.30, pred[4]{0:T(512)(128)(4,1)S(1)} %iota_compare_fusion.4), kind=kOutput, calls=%fused_computation.24 | convolution fusion | flops 13373439 | bytes 2117640 | tf_op jit(solution)/shard_map/dot_general | solution.py:43
  61.5 1.5 collective-permute-done
  63.0 2.0 fusion.7
  65.0 3.9 %multiply_reduce_fusion.2 = (f32[]{:T(128)}, f32[1024,256]{1,0:T(8,128)}) fusion(f32[1024,256]{1,0:T(8,128)S(1)} %fusion.7, f32[256,512]{1,0:T(8,128)} %param.17, f32[256,1024]{0,1:T(8,128)S(1)} %get-tuple-element.42, f32[256,1024]{0,1:T(8,128)} %collective-permute-done, pred[]{:T(512)S(6)} %eq.18), kind=kOutput, calls=%fused_computation.23 | convolution fusion | flops 806354944 | bytes 4456453 | tf_op jit(solution)/shard_map/dot_general | solution.py:61
  68.9 11.2 %all-reduce.1 = (f32[]{:T(128)}, f32[]{:T(128)}) all-reduce(f32[]{:T(128)} %get-tuple-element.41, f32[]{:T(128)} %get-tuple-element.43), channel_id=1, replica_groups=mesh['dp'=8,'tensor'=4] {'tensor'}, use_global_device_ids=true, to_apply=%region_3.4 | all-reduce | flops 2 | bytes 16 | tf_op jit(solution)/shard_map/psum | solution.py:44
  84.2 1.3 multiply_bitcast_fusion.1
  85.5 1.5 collective-permute-start.2
  87.6 22.2 %collective-permute-start.3 = (f32[]{:T(128)}, f32[]{:T(128)}, u32[]{:S(2)}, u32[]{:S(2)}) collective-permute-start(f32[]{:T(128)} %add.112), channel_id=1, source_target_pairs={{0,8},{4,12},{8,0},{12,4},{16,24},{20,28},{24,16},{28,20},{1,9},{5... | collective-permute-start | bytes 20 | tf_op jit(solution)/shard_map/ppermute | solution.py:13
  109.8 1.2 collective-permute-done.3
  112.1 2.3 fusion.4
  114.4 3.5 %multiply_reduce_fusion.1 = (f32[]{:T(128)}, f32[1024,256]{1,0:T(8,128)}) fusion(f32[1024,256]{1,0:T(8,128)S(1)} %fusion.4, f32[256,512]{1,0:T(8,128)} %param.17, f32[256,1024]{0,1:T(8,128)S(1)} %multiply_bitcast_fusion.1, f32[256,1024]{0,1:T(8,128)} %collective-permute-done.2, pred[]{:T(512)S(6)} %eq.17), kind=kOutput, calls=%fused_computation.18 | convolution fusion | flops 806354944 | bytes 4456453 | tf_op jit(solution)/shard_map/dot_general | solution.py:61
  118.0 9.0 %psum.60 = f32[]{:T(128)} all-reduce(f32[]{:T(128)} %get-tuple-element.45), channel_id=1, replica_groups=mesh['dp'=8,'tensor'=4] {'tensor'}, use_global_device_ids=true, to_apply=%region_7.8 | all-reduce | flops 1 | bytes 8 | tf_op jit(solution)/shard_map/psum | solution.py:64
  127.7 1.3 multiply_bitcast_fusion
  129.0 1.5 collective-permute-start.4
  131.8 18.8 %collective-permute-start.5 = (f32[]{:T(128)}, f32[]{:T(128)}, u32[]{:S(2)}, u32[]{:S(2)}) collective-permute-start(f32[]{:T(128)} %add.115), channel_id=1, source_target_pairs={{0,16},{4,20},{8,24},{12,28},{16,0},{20,4},{24,8},{28,12},{1,17},{... | collective-permute-start | bytes 20 | tf_op jit(solution)/shard_map/ppermute | solution.py:13
  150.6 1.1 collective-permute-done.5
  153.1 2.0 fusion.1
  155.1 2.9 multiply_reduce_fusion
  158.0 10.9 %psum.61 = f32[]{:T(128)} all-reduce(f32[]{:T(128)} %get-tuple-element.47), channel_id=1, replica_groups=mesh['dp'=8,'tensor'=4] {'tensor'}, use_global_device_ids=true, to_apply=%region_9.10 | all-reduce | flops 1 | bytes 8 | tf_op jit(solution)/shard_map/psum | solution.py:64
  169.7 2.5 fusion.13
  172.2 1.1 multiply_bitcast_fusion.2
  173.3 2.5 copy.29
  176.5 9.2 %psum.63 = f32[256,4]{0,1:T(4,128)} all-reduce(f32[256,4]{0,1:T(4,128)S(1)} %fusion.11), channel_id=1, replica_groups=mesh['dp'=8,'tensor'=4] {'tensor'}, use_global_device_ids=true, to_apply=%region_16.17 | all-reduce | flops 1024 | bytes 8192 | tf_op jit(solution)/shard_map/psum | solution.py:69
  185.7 20.7 %all-reduce.6.cloned.1.call-done = f32[256,256]{0,1:T(8,128)} async-done(((f32[256,256]{0,1:T(8,128)}), f32[256,256]{0,1:T(8,128)}) %all-reduce.6.cloned.1.call-update) | async-done | bytes 262160 | tf_op jit(solution)/shard_map/psum | solution.py:69
  206.4 1.6 select_reduce_fusion
  208.6 1.0 select_add_fusion
  209.6 0.8 copy.24
  210.5 1.1 fusion.24
  211.5 11.7 %cholesky.49 = f32[128,128]{1,0:T(8,128)S(1)} custom-call(f32[128,128]{1,0:T(8,128)S(1)} %cholesky.115), custom_call_target="Cholesky" | custom-call | tf_op jit(solution)/shard_map/jit(cholesky)/cholesky | solution.py:72
  223.8 10.4 %custom-call.18 = f32[1,128,128]{1,2,0:T(8,128)} custom-call(f32[1,128,128]{2,1,0:T(8,128)S(1)} %get-tuple-element.37), custom_call_target="InvertDiagBlocksLowerTriangular" | custom-call | tf_op jit(solution)/shard_map/jit(cholesky)/cholesky | solution.py:72
  234.3 1.0 fusion.31
  235.3 0.9 convolution_subtract_fusion
  236.2 12.5 %cholesky.103 = f32[128,128]{1,0:T(8,128)S(1)} custom-call(f32[128,128]{1,0:T(8,128)} %convolution_subtract_fusion), custom_call_target="Cholesky" | custom-call | tf_op jit(solution)/shard_map/jit(cholesky)/cholesky | solution.py:72
  249.1 1.4 compare_reduce_fusion
  251.8 1.3 triangular_solve.71
  253.1 6.6 %while.1 = (s32[]{:T(128)}, f32[256,256]{0,1:T(8,128)S(1)}, s32[2,2]{1,0:T(2,128)}, f32[2,128,128]{2,1,0:T(8,128)}, s32[]{:T(128)}) while((s32[]{:T(128)}, f32[256,256]{0,1:T(8,128)S(1)}, s32[2,2]{1,0:T(2,128)}, f32[2,128,128]{2,1,0:T(8,128)}, s32[]{:T(128)}) %tuple.35), condition=%wide.while_cond, body=%wide.while_body.sunk | while | flops 2 | bytes 393829 | solution.py:73
  254.4 1.3 dynamic-slice.7
  257.7 1.3 dynamic-slice.7
  259.7 20.5 %custom-call.19 = f32[2,128,128]{1,2,0:T(8,128)S(1)} custom-call(f32[2,128,128]{2,1,0:T(8,128)} %get-tuple-element.9), custom_call_target="InvertDiagBlocksLowerTriangular" | custom-call | tf_op jit(solution)/shard_map/jit(_cho_solve)/triangular_solve | solution.py:73
  280.2 0.8 fusion.35
  281.0 0.9 convolution_subtract_fusion.3
  282.8 2.2 convolution_subtract_fusion.1
  (49 shorter events, 9.5 us)
Async XLA Ops:
  7.2 1.6 copy-start
  7.2 11.0 %copy-start.2 = (f32[256,1024]{1,0:T(8,128)S(1)}, f32[256,1024]{1,0:T(8,128)}, u32[]{:S(2)}) copy-start(f32[256,1024]{1,0:T(8,128)} %param.15) | copy-start | bytes 3145732
  7.2 50.1 %copy-start.5 = (f32[256,4]{0,1:T(4,128)S(1)}, f32[256,4]{0,1:T(4,128)}, u32[]{:S(2)}) copy-start(f32[256,4]{0,1:T(4,128)} %param.16) | copy-start | bytes 12292
  7.2 48.8 %all-reduce.8.cloned.1.call-start = ((), (), s32[]{:S(2)}) async-start(), calls=%async_computation.1 | async-start | bytes 524288 | tf_op jit(solution)/shard_map/psum | solution.py:33
  10.5 49.7 %copy-start.4 = (s32[8]{0:T(128)S(1)}, s32[8]{0:T(128)}, u32[]{:S(2)}) copy-start(s32[8]{0:T(128)} %param.14) | copy-start | bytes 100
  17.4 189.0 %all-reduce.6.cloned.1.call-start = ((), (), s32[]{:S(2)}) async-start(), calls=%async_computation | async-start | bytes 524288 | tf_op jit(solution)/shard_map/psum | solution.py:69
  19.5 156.4 %copy-start.3 = (pred[4]{0:T(512)(128)(4,1)}, pred[4]{0:T(512)(128)(4,1)S(1)}, u32[]{:S(2)}) copy-start(pred[4]{0:T(512)(128)(4,1)S(1)} %iota_compare_fusion.4) | copy-start | bytes 16
  60.2 2.8 collective-permute-start
  80.1 1.4 collective-permute-start.1
  85.5 26.6 %collective-permute-start.2 = (f32[256,1024]{0,1:T(8,128)S(1)}, f32[256,1024]{0,1:T(8,128)}, u32[]{:S(2)}, u32[]{:S(2)}) collective-permute-start(f32[256,1024]{0,1:T(8,128)S(1)} %multiply_bitcast_fusion.1), channel_id=1, source_target_pairs={{0,8},{4,12},{8,0},{12,4},{16,24},{20,28},{24,16},{28,20},{1,9},{5... | collective-permute-start | bytes 3145736 | tf_op jit(solution)/shard_map/ppermute | solution.py:13
  87.6 23.4 %collective-permute-start.3 = (f32[]{:T(128)}, f32[]{:T(128)}, u32[]{:S(2)}, u32[]{:S(2)}) collective-permute-start(f32[]{:T(128)} %add.112), channel_id=1, source_target_pairs={{0,8},{4,12},{8,0},{12,4},{16,24},{20,28},{24,16},{28,20},{1,9},{5... | collective-permute-start | bytes 20 | tf_op jit(solution)/shard_map/ppermute | solution.py:13
  129.0 24.1 %copy-start.1 = (f32[256,1024]{0,1:T(8,128)}, f32[256,1024]{0,1:T(8,128)S(1)}, u32[]{:S(2)}) copy-start(f32[256,1024]{0,1:T(8,128)S(1)} %multiply_bitcast_fusion) | copy-start | bytes 3145732
  129.0 24.1 %collective-permute-start.4 = (f32[256,1024]{0,1:T(8,128)S(1)}, f32[256,1024]{0,1:T(8,128)}, u32[]{:S(2)}, u32[]{:S(2)}) collective-permute-start(f32[256,1024]{0,1:T(8,128)S(1)} %multiply_bitcast_fusion), channel_id=1, source_target_pairs={{0,16},{4,20},{8,24},{12,28},{16,0},{20,4},{24,8},{28,12},{1,17},{... | collective-permute-start | bytes 3145736 | tf_op jit(solution)/shard_map/ppermute | solution.py:13
  131.8 19.9 %collective-permute-start.5 = (f32[]{:T(128)}, f32[]{:T(128)}, u32[]{:S(2)}, u32[]{:S(2)}) collective-permute-start(f32[]{:T(128)} %add.115), channel_id=1, source_target_pairs={{0,16},{4,20},{8,24},{12,28},{16,0},{20,4},{24,8},{28,12},{1,17},{... | collective-permute-start | bytes 20 | tf_op jit(solution)/shard_map/ppermute | solution.py:13
Sparse Core Ops, SparseCore 0:
  17.6 38.3 all-reduce.7
  172.3 33.9 all-reduce.5
where the time goes:
time: 293 us; the launch traced here: 292 us
  other arithmetic  65.1 us (22%)
  waiting for transfers between devices  61.8 us (21%)
  starting transfers between devices  44.2 us (15%)
  blocking collectives  40.3 us (14%)
  matrix products  38.7 us (13%)
  between operations  26 us (9%)
  local copies, waits for them, and re-layouts  15.8 us (5%)
    ppermute x6, starting transfers between devices, from_partner(): return lax.ppermute(value, axis, pairs)  44.1 us
    another operation x6, other arithmetic, body(): factor = jnp.linalg.cholesky(system)  36.7 us
    psum x1, waiting for transfers between devices, body(): input_side, grad_side = lax.psum((input_part, grad_part), 'tensor')  36.5 us
    another operation x3, other arithmetic, body(): solved = jax.scipy.linalg.cho_solve((factor, True), sketch_grad)  21.1 us
    psum x1, waiting for transfers between devices, body(): gram, sketch_grad = lax.psum((gram_part, product_part), 'tensor')  20.7 us
    psum x2, blocking collectives, body(): mix_total = lax.psum(jnp.sum(mixture * mixture), 'tensor')  19.9 us
    psum x1, blocking collectives, body(): leaf_weight = lax.psum(jnp.sum(leaf_node * leaf_node), 'tensor')  11.2 us
    dot_general x3, matrix products, body(): jnp.dot(mix_first, first, precision=lax.Precision.HIGHEST)  10.4 us
  transfers between devices with their start and end apart: 8, of which 6 were waited for; matrix products, arithmetic and copies ran while one was open for 2% of the time, Pallas kernels for 0%

commit v1 on v0

--- a/solution.py
+++ b/solution.py
@@ -1,10 +1,437 @@
+import functools
+
 import jax
 import jax.numpy as jnp
 from jax import lax
+from jax.experimental import pallas as pl
+from jax.experimental.pallas import tpu as pltpu
 from jax.sharding import PartitionSpec as P
 
 RANK = 64
 SEQ = 128
+LANES = 128
+HIGHEST = lax.Precision.HIGHEST
+MESH = pl.DeviceIdType.MESH
+
+
+def newton_plan(rows):
+    low, high = 0.999, (rows + 1) * 1.001
+    first = 2.0 / (low + high)
+    reach, scales = first * low, []
+    while 1.0 - reach > 1e-4:
+        grown = reach * (2.0 - reach)
+        scale = 2.0 / (1.0 + grown)
+        scales.append(scale)
+        reach = grown * scale
+    return first, scales
+
+
+def dot_high(left, right):
+    return jnp.dot(left, right, precision=HIGHEST, preferred_element_type=jnp.float32)
+
+
+def dot_rows(left, right):
+    return lax.dot_general(
+        left, right, (((1,), (1,)), ((), ())), precision=HIGHEST, preferred_element_type=jnp.float32
+    )
+
+
+def fused_kernel(
+    n_dp,
+    n_tp,
+    act_hbm,
+    out_hbm,
+    wi_hbm,
+    wo_hbm,
+    count_ref,
+    order_ref,
+    prior_hbm,
+    fold_ref,
+    mix_ref,
+    root_out,
+    pre_out,
+    act,
+    outg,
+    wi,
+    wo,
+    prior,
+    zsend,
+    zrecv,
+    full,
+    grads,
+    grads_by_tile,
+    grads_all,
+    sums_z,
+    sums_p,
+    root,
+    gram_part,
+    gram_rs,
+    gram_z,
+    gram,
+    rhs,
+    pre,
+    load_sem,
+    prior_send,
+    prior_recv,
+    z_send,
+    z_recv,
+    p_send,
+    p_recv,
+    out_sem,
+):
+    f32 = jnp.float32
+    me, z = lax.axis_index("dp"), lax.axis_index("tensor")
+    rows = gram.shape[0]
+    block = rows // n_dp
+    levels = n_dp.bit_length() - 1
+
+    def dp_of(k):
+        return lax.rem(me + k, n_dp)
+
+    def tp_of(k):
+        return lax.rem(z + k, n_tp)
+
+    order = sorted(range(1, n_tp), key=lambda k: -min(k, n_tp - k)) + [0]
+    loads = []
+    for index, (src, dst) in enumerate(((wi_hbm, wi), (wo_hbm, wo))):
+        loads.append(pltpu.make_async_copy(src, dst, load_sem.at[index]))
+        loads[-1].start()
+    chunk_loads = []
+    for index, k in enumerate(order):
+        e = tp_of(k)
+        span = pl.ds(pl.multiple_of(e * SEQ, SEQ), SEQ)
+        pair = (
+            pltpu.make_async_copy(act_hbm.at[span], act.at[index], load_sem.at[2 + 2 * index]),
+            pltpu.make_async_copy(out_hbm.at[span], outg.at[index], load_sem.at[3 + 2 * index]),
+        )
+        for copy in pair:
+            copy.start()
+        chunk_loads.append(pair)
+
+    def tile_of(owner):
+        return pl.ds(pl.multiple_of(owner * LANES, LANES), LANES)
+
+    own_prior = pltpu.make_async_copy(
+        prior_hbm.at[:, tile_of(me)], prior.at[me], load_sem.at[2 + 2 * n_tp]
+    )
+    own_prior.start()
+
+    barrier = pltpu.get_barrier_semaphore()
+    for k in range(1, n_dp):
+        pl.semaphore_signal(barrier, inc=1, device_id={"dp": dp_of(k)}, device_id_type=MESH)
+    for k in range(1, n_tp):
+        pl.semaphore_signal(barrier, inc=1, device_id={"tensor": tp_of(k)}, device_id_type=MESH)
+    pl.semaphore_wait(barrier, n_dp + n_tp - 2)
+
+    prior_copies = []
+    for k in range(1, n_dp):
+        prior_copies.append(
+            pltpu.make_async_remote_copy(
+                src_ref=prior_hbm.at[:, tile_of(dp_of(k))],
+                dst_ref=prior.at[me],
+                send_sem=prior_send.at[k],
+                recv_sem=prior_recv.at[k],
+                device_id={"dp": dp_of(k)},
+                device_id_type=MESH,
+            )
+        )
+        prior_copies[-1].start()
+
+    def exchange(axis, phase, source, target):
+        size, other = (n_tp, tp_of) if axis == "tensor" else (n_dp, dp_of)
+        send, recv = (z_send, z_recv) if axis == "tensor" else (p_send, p_recv)
+        copies = []
+        for k in range(1, size):
+            copies.append(
+                pltpu.make_async_remote_copy(
+                    src_ref=source(other(k)),
+                    dst_ref=target,
+                    send_sem=send.at[phase, k],
+                    recv_sem=recv.at[phase, k],
+                    device_id={axis: other(k)},
+                    device_id_type=MESH,
+                )
+            )
+            copies[-1].start()
+        return copies
+
+    for copy in loads:
+        copy.wait()
+    side_copies = []
+    for index, k in enumerate(order):
+        for copy in chunk_loads[index]:
+            copy.wait()
+        left = jnp.dot(act[index], wi[...], preferred_element_type=f32)
+        right = jnp.dot(outg[index], wo[...], preferred_element_type=f32)
+        both = jnp.concatenate([left, right], axis=1)
+        if k == 0:
+            zrecv[z] = both
+        else:
+            zsend[index] = both
+            copy = pltpu.make_async_remote_copy(
+                src_ref=zsend.at[index],
+                dst_ref=zrecv.at[z],
+                send_sem=z_send.at[0, k],
+                recv_sem=z_recv.at[0, k],
+                device_id={"tensor": tp_of(k)},
+                device_id_type=MESH,
+            )
+            copy.start()
+            side_copies.append(copy)
+    for copy in side_copies:
+        copy.wait()
+    sides = zrecv[0]
+    for index in range(1, n_tp):
+        sides = sides + zrecv[index]
+    lane = lax.broadcasted_iota(jnp.int32, sides.shape, 1)
+    doubled = jnp.where(lane < RANK, sides, pltpu.roll(sides, RANK, 1))
+    product = dot_high(sides.T, doubled) / jnp.sqrt(f32(SEQ))
+    product = jnp.where(z < count_ref[0], product, jnp.zeros_like(product))
+    full[...] = product[RANK:]
+    even = full[pl.ds(0, RANK // 2, stride=2), :]
+    odd = full[pl.ds(1, RANK // 2, stride=2), :]
+    lane = lax.broadcasted_iota(jnp.int32, even.shape, 1)
+    mine = jnp.where(lane < RANK, even, odd)
+    for index in range(n_tp):
+        zsend[n_tp + index, 0:n_dp, :] = mine[index * n_dp : (index + 1) * n_dp]
+    grads[z] = zsend[n_tp + z, 0:n_dp, :]
+    for copy in exchange("tensor", 1, lambda t: zsend.at[n_tp + t, 0:n_dp, :], grads.at[z]):
+        copy.wait()
+    for index in range(n_tp):
+        value = grads[index]
+        for tile in range(n_dp):
+            grads_by_tile[tile, index : index + 1, :] = value[tile : tile + 1]
+    grads_all[me] = grads_by_tile[me]
+    grad_copies = exchange("dp", 0, lambda t: grads_by_tile.at[t], grads_all.at[me])
+    own_prior.wait()
+    for copy in prior_copies:
+        copy.wait()
+    for copy in grad_copies:
+        copy.wait()
+
+    fold = fold_ref[...]
+    sums = []
+
+    def total(value):
+        sums.append(jnp.sum(jnp.sum(value, axis=0, keepdims=True), axis=1, keepdims=True))
+        return len(sums) - 1
+
+    leaves, leaf_mass = [], []
+    for r in range(n_dp):
+        leaf = prior[r]
+        step = grads_all[r]
+        for e in range(n_tp):
+            leaf = leaf + fold[:, e : e + 1] * step[e : e + 1, :]
+        leaf_mass.append(total(leaf * leaf))
+        leaves.append([leaf])
+    first_mix, second_mix = mix_ref[:, :rows], mix_ref[:, rows:]
+    nodes, products, flags = leaves, [], []
+    for level in range(levels):
+        merged, level_products, level_flags = [], [], []
+        for j in range(len(nodes) // 2):
+            flip = order_ref[j * 2 ** (level + 1) + 2**level - 1] == 1
+            level_flags.append(flip)
+            lower, upper = nodes[2 * j], nodes[2 * j + 1]
+            first = [jnp.where(flip, b, a) for a, b in zip(lower, upper)]
+            second = [jnp.where(flip, a, b) for a, b in zip(lower, upper)]
+            parts = [dot_high(first_mix, a) for a in first] + [dot_high(second_mix, a) for a in second]
+            if level == 0:
+                parts = [parts[0] + parts[1]]
+            merged.append(parts)
+            level_products.append(
+                {(a, b): total(parts[a] * parts[b]) for a in range(len(parts)) for b in range(a + 1)}
+            )
+        nodes = merged
+        products.append(level_products)
+        flags.append(level_flags)
+    lane = lax.broadcasted_iota(jnp.int32, (8, LANES), 1)
+    packed = jnp.zeros((8, LANES), f32)
+    for index, value in enumerate(sums):
+        packed = jnp.where(lane == index, value, packed)
+    sums_z[z] = packed
+    for copy in exchange("tensor", 2, lambda t: sums_z.at[z], sums_z.at[z]):
+        copy.wait()
+    packed = sums_z[0]
+    for index in range(1, n_tp):
+        packed = packed + sums_z[index]
+    sums_p[me] = packed
+    for copy in exchange("dp", 1, lambda t: sums_p.at[me], sums_p.at[me]):
+        copy.wait()
+    packed = sums_p[0]
+    for index in range(1, n_dp):
+        packed = packed + sums_p[index]
+    packed = packed[0:1]
+    lane = lax.broadcasted_iota(jnp.int32, (1, LANES), 1)
+
+    def summed(index):
+        return jnp.sum(jnp.where(lane == index, packed, 0.0), axis=1, keepdims=True)
+
+    masses = [summed(index) for index in leaf_mass]
+    scales = [[jnp.ones((1, 1), f32)] for _ in range(n_dp)]
+    for level in range(levels):
+        new_masses, new_scales = [], []
+        for j, products_of in enumerate(products[level]):
+            flip = flags[level][j]
+            lower, upper = scales[2 * j], scales[2 * j + 1]
+            if level == 0:
+                coefs = [jnp.ones((1, 1), f32)]
+            else:
+                coefs = [jnp.where(flip, b, a) for a, b in zip(lower, upper)]
+                coefs += [jnp.where(flip, a, b) for a, b in zip(lower, upper)]
+            square = jnp.zeros((1, 1), f32)
+            for (a, b), index in products_of.items():
+                term = coefs[a] * (coefs[b] * summed(index))
+                square = square + (term if a == b else 2.0 * term)
+            mass = masses[2 * j] + masses[2 * j + 1]
+            scale = jnp.sqrt(mass / (jnp.maximum(square, 0.0) + 1e-06))
+            new_masses.append(mass)
+            new_scales.append([scale * c for c in coefs])
+        masses, scales = new_masses, new_scales
+    chunk = scales[0][0] * nodes[0][0]
+    for c, part in zip(scales[0][1:], nodes[0][1:]):
+        chunk = chunk + c * part
+    root[:, tile_of(me)] = chunk
+
+    gram_part[...] = dot_rows(chunk, chunk)
+
+    def rows_of(owner):
+        return pl.ds(pl.multiple_of(owner * block, block), block)
+
+    gram_rs[me] = gram_part[rows_of(me), :]
+    gram_copies = exchange("dp", 2, lambda t: gram_part.at[rows_of(t)], gram_rs.at[me])
+    root_copies = exchange("dp", 3, lambda t: root.at[:, tile_of(me)], root.at[:, tile_of(me)])
+    for copy in gram_copies:
+        copy.wait()
+    part = gram_rs[0]
+    for index in range(1, n_dp):
+        part = part + gram_rs[index]
+    gram_z[z] = part
+    for copy in exchange("tensor", 3, lambda t: gram_z.at[z], gram_z.at[z]):
+        copy.wait()
+    part = gram_z[0]
+    for index in range(1, n_tp):
+        part = part + gram_z[index]
+    gram[rows_of(me), :] = part
+    gram_copies = exchange("dp", 4, lambda t: gram.at[rows_of(me)], gram.at[rows_of(me)])
+    for copy in root_copies:
+        copy.wait()
+    root_write = pltpu.make_async_copy(root, root_out, out_sem.at[0])
+    root_write.start()
+    for index in range(n_tp):
+        value = grads[index]
+        for tile in range(n_dp):
+            pre[index : index + 1, tile * LANES : (tile + 1) * LANES] = value[tile : tile + 1]
+    rhs[z] = dot_rows(pre[...], root[...])
+    rhs_copies = exchange("tensor", 4, lambda t: rhs.at[z], rhs.at[z])
+    for copy in gram_copies:
+        copy.wait()
+
+    system = gram[...]
+    eye = lax.broadcasted_iota(jnp.int32, system.shape, 0) == lax.broadcasted_iota(
+        jnp.int32, system.shape, 1
+    )
+    trace = jnp.sum(
+        jnp.sum(jnp.where(eye, system, 0.0), axis=0, keepdims=True), axis=1, keepdims=True
+    )
+    damping = trace / rows
+    unit = 1.0 / damping
+    system = system * unit + jnp.where(eye, 1.0, 0.0)
+    first, steps = newton_plan(rows)
+    inverse = None
+    for scale in steps:
+        if inverse is None:
+            inverse = jnp.where(eye, 2.0 * first * scale, 0.0) - (first * first * scale) * system
+        else:
+            residual = jnp.where(eye, 2.0, 0.0) - dot_high(system, inverse)
+            inverse = scale * dot_high(inverse, residual)
+    for copy in rhs_copies:
+        copy.wait()
+    target = rhs[0]
+    for index in range(1, n_tp):
+        target = target + rhs[index]
+    target = target * unit
+    solved = dot_rows(target, inverse)
+    for _ in range(2):
+        solved = solved + dot_rows(target - dot_rows(solved, system), inverse)
+    pre[...] = pre[...] - dot_high(solved, root[...])
+    pre_write = pltpu.make_async_copy(pre, pre_out, out_sem.at[1])
+    pre_write.start()
+    pre_write.wait()
+    root_write.wait()
+
+
+def fused_body(
+    activations,
+    out_grads,
+    input_proj,
+    grad_proj,
+    example_count,
+    child_order,
+    prior_sketch,
+    fold_map,
+    merge_mix,
+):
+    n_dp, n_tp = lax.axis_size("dp"), lax.axis_size("tensor")
+    rows, columns = prior_sketch.shape
+    slots = activations.shape[0] // SEQ
+    f32, bf16 = jnp.float32, jnp.bfloat16
+    width, hidden = activations.shape[1], out_grads.shape[1]
+    phases = 5
+    hbm = pl.BlockSpec(memory_space=pl.ANY)
+    vmem = pl.BlockSpec(memory_space=pltpu.VMEM)
+    smem = pl.BlockSpec(memory_space=pltpu.SMEM)
+    return pl.pallas_call(
+        functools.partial(fused_kernel, n_dp, n_tp),
+        out_shape=(
+            jax.ShapeDtypeStruct((rows, columns), f32),
+            jax.ShapeDtypeStruct((slots, columns), f32),
+        ),
+        in_specs=[hbm, hbm, hbm, hbm, smem, smem, hbm, vmem, vmem],
+        out_specs=(hbm, hbm),
+        scratch_shapes=[
+            pltpu.VMEM((slots, SEQ, width), bf16),
+            pltpu.VMEM((slots, SEQ, hidden), bf16),
+            pltpu.VMEM(input_proj.shape, bf16),
+            pltpu.VMEM(grad_proj.shape, bf16),
+            pltpu.VMEM((n_dp, rows, LANES), f32),
+            pltpu.VMEM((2 * n_tp, SEQ, LANES), f32),
+            pltpu.VMEM((n_tp, SEQ, LANES), f32),
+            pltpu.VMEM((RANK, LANES), f32),
+            pltpu.VMEM((n_tp, n_dp, LANES), f32),
+            pltpu.VMEM((n_dp, n_tp, LANES), f32),
+            pltpu.VMEM((n_dp, n_tp, LANES), f32),
+            pltpu.VMEM((n_tp, 8, LANES), f32),
+            pltpu.VMEM((n_dp, 8, LANES), f32),
+            pltpu.VMEM((rows, columns), f32),
+            pltpu.VMEM((rows, rows), f32),
+            pltpu.VMEM((n_dp, rows // n_dp, rows), f32),
+            pltpu.VMEM((n_tp, rows // n_dp, rows), f32),
+            pltpu.VMEM((rows, rows), f32),
+            pltpu.VMEM((n_tp, slots, rows), f32),
+            pltpu.VMEM((slots, columns), f32),
+            pltpu.SemaphoreType.DMA((3 + 2 * n_tp,)),
+            pltpu.SemaphoreType.DMA((n_dp,)),
+            pltpu.SemaphoreType.DMA((n_dp,)),
+            pltpu.SemaphoreType.DMA((phases, n_tp)),
+            pltpu.SemaphoreType.DMA((phases, n_tp)),
+            pltpu.SemaphoreType.DMA((phases, n_dp)),
+            pltpu.SemaphoreType.DMA((phases, n_dp)),
+            pltpu.SemaphoreType.DMA((2,)),
+        ],
+        compiler_params=pltpu.CompilerParams(
+            collective_id=0, has_side_effects=True, vmem_limit_bytes=56 * 2**20
+        ),
+    )(
+        activations,
+        out_grads,
+        input_proj,
+        grad_proj,
+        example_count,
+        child_order,
+        prior_sketch,
+        fold_map,
+        merge_mix,
+    )
 
 
 def from_partner(value, axis, stride):
@@ -75,6 +502,26 @@
     return (sketch_node, preconditioned)
 
 
+def fits_fused(rows, columns, slots, n_dp, n_tp):
+    return (
+        columns == n_dp * LANES
+        and slots == n_tp
+        and 2 * RANK == LANES
+        and n_dp == 2 ** (n_dp.bit_length() - 1)
+        and n_dp % 8 == 0
+        and rows % (8 * n_dp) == 0
+    )
+
+
+def step(*args):
+    n_dp, n_tp = lax.axis_size("dp"), lax.axis_size("tensor")
+    slots = args[0].shape[0] // SEQ
+    rows, columns = args[6].shape
+    if fits_fused(rows, columns, slots, n_dp, n_tp):
+        return fused_body(*args)
+    return body(*args)
+
+
 def solution(mesh):
     in_specs = (
         P("dp", "tensor"),
@@ -88,4 +535,4 @@
         P(),
     )
     out_specs = (P(None, "tensor"), P("dp", "tensor"))
-    return jax.shard_map(body, mesh=mesh, in_specs=in_specs, out_specs=out_specs, check_vma=False)
+    return jax.shard_map(step, mesh=mesh, in_specs=in_specs, out_specs=out_specs, check_vma=False)

time: 293 us -> 73.6 us (0.25)
  other arithmetic: 65.1 us -> 0 us
  Pallas kernels: 0 us -> 63.1 us
  waiting for transfers between devices: 61.8 us -> 0 us
  starting transfers between devices: 44.2 us -> 0 us
  blocking collectives: 40.3 us -> 0 us
  matrix products: 38.7 us -> 0 us
  between operations: 26 us -> 1.3 us
  local copies, waits for them, and re-layouts: 15.8 us -> 8.96 us
    pallas_call x0 -> x1, Pallas kernels: none -> 63.1 us  [fused_body(): pl.pallas_call(functools.partial(fused_kernel, n_dp, n_tp), out_shape=(ja...]
    another operation x9 -> x0, other arithmetic: 57.8 us -> none  [the longest x6 36.7 us: body(): factor = jnp.linalg.cholesky(system)]
    psum x2 -> x0, waiting for transfers between devices: 57.2 us -> none  [the longest x1 36.5 us: body(): input_side, grad_side = lax.psum((input_part, grad_part), 'tensor')]
    ppermute x6 -> x0, starting transfers between devices: 44.1 us -> none  [from_partner(): return lax.ppermute(value, axis, pairs)]
    psum x4 -> x0, blocking collectives: 40.3 us -> none  [the longest x2 19.9 us: body(): mix_total = lax.psum(jnp.sum(mixture * mixture), 'tensor')]
    dot_general x13 -> x0, matrix products: 34.1 us -> none  [the longest x3 10.4 us: body(): jnp.dot(mix_first, first, precision=lax.Precision.HIGHEST)]
    another operation x18 -> x0, local copies, waits for them, and re-layouts: 8.16 us -> none
    another operation x8 -> x0, matrix products: 4.58 us -> none  [the longest x6 2.65 us: body(): solved = jax.scipy.linalg.cho_solve((factor, True), sketch_grad)]
  transfers between devices with their start and end apart: 8 -> 0, of which waited for: 6 -> 0; matrix products, arithmetic and copies ran while one was open for 2% -> 0% of each run, Pallas kernels for 0% -> 0%
where the time goes in v1:
time: 73.6 us; the launch traced here: 73.3 us
  Pallas kernels  63.1 us (86%)
  local copies, waits for them, and re-layouts  8.96 us (12%)
  between operations  1.3 us (2%)
    pallas_call x1, Pallas kernels, fused_body(): pl.pallas_call(functools.partial(fused_kernel, n_dp, n_tp), out_shape=(ja...  63.1 us
    unnamed x7, local copies, waits for them, and re-layouts  8.96 us

profile of v1, /device:TPU:0, one launch (start us, length us, event | category | flops | bytes accessed | tf_op | source)
XLA Modules:
  0.0 73.3 jit_solution(14421351319759252704)
XLA Ops:
  1.3 1.5 %copy.13.fold_ref = f32[256,4]{1,0:T(8,128)} copy(f32[256,4]{0,1:T(4,128)} %param.16) | data formatting | bytes 8192 | tf_op args[7]
  2.8 2.0 %copy.11.wi_hbm = bf16[2048,64]{1,0:T(8,128)(2,1)} copy(bf16[2048,64]{0,1:T(8,128)(2,1)} %param.11) | data formatting | bytes 524288 | tf_op args[2]
  4.7 2.6 %copy.12.wo_hbm = bf16[7168,64]{1,0:T(8,128)(2,1)} copy(bf16[7168,64]{0,1:T(8,128)(2,1)} %param.12) | data formatting | bytes 1835008 | tf_op args[3]
  7.3 63.1 %shard_map.104 = (f32[256,1024]{1,0:T(8,128)}, f32[4,1024]{1,0:T(4,128)}) custom-call(bf16[512,2048]{1,0:T(8,128)(2,1)} %act_hbm.1, bf16[512,7168]{1,0:T(8,128)(2,1)} %out_hbm.1, bf16[2048,64]{1,0:T(8,128)(2,1)} %copy.11.wi_hbm, bf16[7168,64]{1,0:T(8,128)(2,1)} %copy.12.wo_hbm, s32[1]{0:T(128)S(6)} %copy.16.count_ref, s32[8]{0:T(128)} %order_ref.1, ...), custom_call_target="tpu_custom_call" | custom-call | tf_op jit(solution)/shard_map/pallas_call | solution.py:383
  70.4 0.0 copy-start
  70.4 2.3 %copy.17 = f32[256,1024]{1,0:T(8,128)} copy(f32[256,1024]{1,0:T(8,128)} %get-tuple-element.4) | data formatting | bytes 2097152
  72.7 0.0 copy-done
  72.7 0.6 copy.18
Async XLA Ops:
  70.4 2.3 %copy-start = (f32[4,1024]{1,0:T(4,128)S(1)}, f32[4,1024]{1,0:T(4,128)}, u32[]{:S(2)}) copy-start(f32[4,1024]{1,0:T(4,128)} %get-tuple-element.5) | copy-start | bytes 49156

commit v2 on v1

--- a/solution.py
+++ b/solution.py
@@ -18,7 +18,7 @@
     low, high = 0.999, (rows + 1) * 1.001
     first = 2.0 / (low + high)
     reach, scales = first * low, []
-    while 1.0 - reach > 1e-4:
+    while 1.0 - reach > 1e-3:
         grown = reach * (2.0 - reach)
         scale = 2.0 / (1.0 + grown)
         scales.append(scale)
@@ -30,10 +30,26 @@
     return jnp.dot(left, right, precision=HIGHEST, preferred_element_type=jnp.float32)
 
 
+def dot_flip(left, right):
+    return lax.dot_general(left, right, (((1,), (1,)), ((), ())), preferred_element_type=jnp.float32)
+
+
 def dot_rows(left, right):
     return lax.dot_general(
         left, right, (((1,), (1,)), ((), ())), precision=HIGHEST, preferred_element_type=jnp.float32
     )
+
+
+def halves(value):
+    high = value.astype(jnp.bfloat16)
+    return high, (value - high.astype(jnp.float32)).astype(jnp.bfloat16)
+
+
+def dot_halves(left, right):
+    (a, b), (c, d) = left, right
+    out = jnp.dot(a, c, preferred_element_type=jnp.float32)
+    out = out + jnp.dot(a, d, preferred_element_type=jnp.float32)
+    return out + jnp.dot(b, c, preferred_element_type=jnp.float32)
 
 
 def fused_kernel(
@@ -49,7 +65,9 @@
     fold_ref,
     mix_ref,
     root_out,
-    pre_out,
+    gram_out,
+    rhs_out,
+    grads_out,
     act,
     outg,
     wi,
@@ -68,8 +86,6 @@
     gram_rs,
     gram_z,
     gram,
-    rhs,
-    pre,
     load_sem,
     prior_send,
     prior_recv,
@@ -83,6 +99,7 @@
     me, z = lax.axis_index("dp"), lax.axis_index("tensor")
     rows = gram.shape[0]
     block = rows // n_dp
+    part_rows = gram_z.shape[1]
     levels = n_dp.bit_length() - 1
 
     def dp_of(k):
@@ -161,8 +178,8 @@
     for index, k in enumerate(order):
         for copy in chunk_loads[index]:
             copy.wait()
-        left = jnp.dot(act[index], wi[...], preferred_element_type=f32)
-        right = jnp.dot(outg[index], wo[...], preferred_element_type=f32)
+        left = dot_flip(act[index], wi[...])
+        right = dot_flip(outg[index], wo[...])
         both = jnp.concatenate([left, right], axis=1)
         if k == 0:
             zrecv[z] = both
@@ -209,7 +226,7 @@
     for copy in grad_copies:
         copy.wait()
 
-    fold = fold_ref[...]
+    fold = fold_ref[...].T
     sums = []
 
     def total(value):
@@ -292,14 +309,20 @@
         chunk = chunk + c * part
     root[:, tile_of(me)] = chunk
 
-    gram_part[...] = dot_rows(chunk, chunk)
-
-    def rows_of(owner):
-        return pl.ds(pl.multiple_of(owner * block, block), block)
-
-    gram_rs[me] = gram_part[rows_of(me), :]
-    gram_copies = exchange("dp", 2, lambda t: gram_part.at[rows_of(t)], gram_rs.at[me])
+    square = dot_rows(chunk, chunk)
+    every = jnp.concatenate([grads_all[r] for r in range(n_dp)], axis=0)
+    targets = dot_rows(every, chunk)
+    filler = jnp.zeros((part_rows - block - n_tp, rows), f32)
+    for r in range(n_dp):
+        gram_part[r, 0:block, :] = square[r * block : (r + 1) * block]
+        gram_part[r, block:, :] = jnp.concatenate([targets[r * n_tp : (r + 1) * n_tp], filler], axis=0)
+    gram_rs[me] = gram_part[me]
+    gram_copies = exchange("dp", 2, lambda t: gram_part.at[t], gram_rs.at[me])
     root_copies = exchange("dp", 3, lambda t: root.at[:, tile_of(me)], root.at[:, tile_of(me)])
+    for index in range(n_tp):
+        value = grads[index]
+        for tile in range(n_dp):
+            grads_out[index : index + 1, tile * LANES : (tile + 1) * LANES] = value[tile : tile + 1]
     for copy in gram_copies:
         copy.wait()
     part = gram_rs[0]
@@ -311,53 +334,49 @@
     part = gram_z[0]
     for index in range(1, n_tp):
         part = part + gram_z[index]
-    gram[rows_of(me), :] = part
-    gram_copies = exchange("dp", 4, lambda t: gram.at[rows_of(me)], gram.at[rows_of(me)])
+    own_rows = pl.ds(pl.multiple_of(me * block, block), block)
+    gram[own_rows, :] = part[0:block]
+    gram_copies = exchange("dp", 4, lambda t: gram.at[own_rows], gram.at[own_rows])
+    rhs_out[...] = part[block : block + n_tp]
     for copy in root_copies:
         copy.wait()
     root_write = pltpu.make_async_copy(root, root_out, out_sem.at[0])
     root_write.start()
-    for index in range(n_tp):
-        value = grads[index]
-        for tile in range(n_dp):
-            pre[index : index + 1, tile * LANES : (tile + 1) * LANES] = value[tile : tile + 1]
-    rhs[z] = dot_rows(pre[...], root[...])
-    rhs_copies = exchange("tensor", 4, lambda t: rhs.at[z], rhs.at[z])
     for copy in gram_copies:
         copy.wait()
-
-    system = gram[...]
+    gram_out[...] = gram[...]
+    root_write.wait()
+
+
+def solve_kernel(root_hbm, gram_ref, rhs_ref, grads_ref, root_out, pre_out, root, sems):
+    read = pltpu.make_async_copy(root_hbm, root, sems.at[0])
+    read.start()
+    system = gram_ref[...]
+    rows = system.shape[0]
     eye = lax.broadcasted_iota(jnp.int32, system.shape, 0) == lax.broadcasted_iota(
         jnp.int32, system.shape, 1
     )
     trace = jnp.sum(
         jnp.sum(jnp.where(eye, system, 0.0), axis=0, keepdims=True), axis=1, keepdims=True
     )
-    damping = trace / rows
-    unit = 1.0 / damping
+    unit = 1.0 / (trace / rows)
     system = system * unit + jnp.where(eye, 1.0, 0.0)
+    system_halves = halves(system)
     first, steps = newton_plan(rows)
-    inverse = None
-    for scale in steps:
-        if inverse is None:
-            inverse = jnp.where(eye, 2.0 * first * scale, 0.0) - (first * first * scale) * system
-        else:
-            residual = jnp.where(eye, 2.0, 0.0) - dot_high(system, inverse)
-            inverse = scale * dot_high(inverse, residual)
-    for copy in rhs_copies:
-        copy.wait()
-    target = rhs[0]
-    for index in range(1, n_tp):
-        target = target + rhs[index]
-    target = target * unit
+    inverse = jnp.where(eye, 2.0 * first * steps[0], 0.0) - (first * first * steps[0]) * system
+    for scale in steps[1:]:
+        inverse_halves = halves(inverse)
+        residual = jnp.where(eye, 2.0, 0.0) - dot_halves(system_halves, inverse_halves)
+        inverse = scale * dot_halves(inverse_halves, halves(residual))
+    read.wait()
+    write = pltpu.make_async_copy(root, root_out, sems.at[1])
+    write.start()
+    target = rhs_ref[...] * unit
     solved = dot_rows(target, inverse)
     for _ in range(2):
         solved = solved + dot_rows(target - dot_rows(solved, system), inverse)
-    pre[...] = pre[...] - dot_high(solved, root[...])
-    pre_write = pltpu.make_async_copy(pre, pre_out, out_sem.at[1])
-    pre_write.start()
-    pre_write.wait()
-    root_write.wait()
+    pre_out[...] = grads_ref[...] - dot_high(solved, root[...])
+    write.wait()
 
 
 def fused_body(
@@ -380,19 +399,22 @@
     hbm = pl.BlockSpec(memory_space=pl.ANY)
     vmem = pl.BlockSpec(memory_space=pltpu.VMEM)
     smem = pl.BlockSpec(memory_space=pltpu.SMEM)
-    return pl.pallas_call(
+    part_rows = -(-(rows // n_dp + slots) // 8) * 8
+    root, gram, rhs, grads = pl.pallas_call(
         functools.partial(fused_kernel, n_dp, n_tp),
         out_shape=(
             jax.ShapeDtypeStruct((rows, columns), f32),
+            jax.ShapeDtypeStruct((rows, rows), f32),
+            jax.ShapeDtypeStruct((slots, rows), f32),
             jax.ShapeDtypeStruct((slots, columns), f32),
         ),
         in_specs=[hbm, hbm, hbm, hbm, smem, smem, hbm, vmem, vmem],
-        out_specs=(hbm, hbm),
+        out_specs=(hbm, vmem, vmem, vmem),
         scratch_shapes=[
             pltpu.VMEM((slots, SEQ, width), bf16),
             pltpu.VMEM((slots, SEQ, hidden), bf16),
-            pltpu.VMEM(input_proj.shape, bf16),
-            pltpu.VMEM(grad_proj.shape, bf16),
+            pltpu.VMEM((RANK, width), bf16),
+            pltpu.VMEM((RANK, hidden), bf16),
             pltpu.VMEM((n_dp, rows, LANES), f32),
             pltpu.VMEM((2 * n_tp, SEQ, LANES), f32),
             pltpu.VMEM((n_tp, SEQ, LANES), f32),
@@ -403,12 +425,10 @@
             pltpu.VMEM((n_tp, 8, LANES), f32),
             pltpu.VMEM((n_dp, 8, LANES), f32),
             pltpu.VMEM((rows, columns), f32),
+            pltpu.VMEM((n_dp, part_rows, rows), f32),
+            pltpu.VMEM((n_dp, part_rows, rows), f32),
+            pltpu.VMEM((n_tp, part_rows, rows), f32),
             pltpu.VMEM((rows, rows), f32),
-            pltpu.VMEM((n_dp, rows // n_dp, rows), f32),
-            pltpu.VMEM((n_tp, rows // n_dp, rows), f32),
-            pltpu.VMEM((rows, rows), f32),
-            pltpu.VMEM((n_tp, slots, rows), f32),
-            pltpu.VMEM((slots, columns), f32),
             pltpu.SemaphoreType.DMA((3 + 2 * n_tp,)),
             pltpu.SemaphoreType.DMA((n_dp,)),
             pltpu.SemaphoreType.DMA((n_dp,)),
@@ -416,7 +436,7 @@
             pltpu.SemaphoreType.DMA((phases, n_tp)),
             pltpu.SemaphoreType.DMA((phases, n_dp)),
             pltpu.SemaphoreType.DMA((phases, n_dp)),
-            pltpu.SemaphoreType.DMA((2,)),
+            pltpu.SemaphoreType.DMA((1,)),
         ],
         compiler_params=pltpu.CompilerParams(
             collective_id=0, has_side_effects=True, vmem_limit_bytes=56 * 2**20
@@ -424,14 +444,25 @@
     )(
         activations,
         out_grads,
-        input_proj,
-        grad_proj,
+        input_proj.T,
+        grad_proj.T,
         example_count,
         child_order,
         prior_sketch,
-        fold_map,
+        fold_map.T,
         merge_mix,
     )
+    return pl.pallas_call(
+        solve_kernel,
+        out_shape=(
+            jax.ShapeDtypeStruct((rows, columns), f32),
+            jax.ShapeDtypeStruct((slots, columns), f32),
+        ),
+        in_specs=[hbm, vmem, vmem, vmem],
+        out_specs=(hbm, vmem),
+        scratch_shapes=[pltpu.VMEM((rows, columns), f32), pltpu.SemaphoreType.DMA((2,))],
+        compiler_params=pltpu.CompilerParams(vmem_limit_bytes=56 * 2**20),
+    )(root, gram, rhs, grads)
 
 
 def from_partner(value, axis, stride):

time: 73.6 us -> 64.8 us (0.88)
  local copies, waits for them, and re-layouts: 8.96 us -> 0 us
    unnamed x7 -> x0, local copies, waits for them, and re-layouts: 8.96 us -> none
    pallas_call x0 -> x1, Pallas kernels: none -> 8.04 us  [fused_body(): pl.pallas_call(solve_kernel, out_shape=(jax.ShapeDtypeStruct((rows, colum...]
    pallas_call x1, Pallas kernels: 63.1 us -> 55.3 us  [fused_body(): pl.pallas_call(functools.partial(fused_kernel, n_dp, n_tp), out_shape=(ja...]
where the time goes in v2:
time: 64.8 us; the launch traced here: 64.6 us
  Pallas kernels  63.3 us (98%)
  between operations  1.29 us (2%)
    pallas_call x1, Pallas kernels, fused_body(): pl.pallas_call(functools.partial(fused_kernel, n_dp, n_tp), out_shape=(ja...  55.3 us
    pallas_call x1, Pallas kernels, fused_body(): pl.pallas_call(solve_kernel, out_shape=(jax.ShapeDtypeStruct((rows, colum...  8.04 us

profile of v2, /device:TPU:0, one launch (start us, length us, event | category | flops | bytes accessed | tf_op | source)
XLA Modules:
  0.0 64.6 jit_solution(16035944321829700518)
XLA Ops:
  1.3 55.3 %shard_map.104 = (f32[256,1024]{1,0:T(8,128)}, f32[256,256]{1,0:T(8,128)}, f32[4,256]{1,0:T(4,128)}, f32[4,1024]{1,0:T(4,128)}) custom-call(bf16[512,2048]{1,0:T(8,128)(2,1)} %act_hbm.1, bf16[512,7168]{1,0:T(8,128)(2,1)} %out_hbm.1, bf16[64,2048]{1,0:T(8,128)(2,1)} %bitcast.4, bf16[64,7168]{1,0:T(8,128)(2,1)} %bitcast.3, s32[1]{0:T(128)S(6)} %copy.11.count_ref, ...), custom_call_target="tpu_custom_call" | custom-call | tf_op jit(solution)/shard_map/pallas_call | solution.py:403
  56.5 8.0 %shard_map.105 = (f32[256,1024]{1,0:T(8,128)}, f32[4,1024]{1,0:T(4,128)}) custom-call(f32[256,1024]{1,0:T(8,128)} %get-tuple-element.6.root_hbm, f32[256,256]{1,0:T(8,128)} %get-tuple-element.7.gram_ref, f32[4,256]{1,0:T(4,128)} %get-tuple-element.8.rhs_ref, f32[4,1024]{1,0:T(4,128)} %get-tuple-element.9.grads_ref), custom_call_target="tpu_custom_call" | custom-call | tf_op jit(solution)/shard_map/pallas_call | solution.py:455

commit v3 on v2

--- a/solution.py
+++ b/solution.py
@@ -73,6 +73,9 @@
     wi,
     wo,
     prior,
+    pair_in,
+    node_send,
+    node_recv,
     zsend,
     zrecv,
     full,
@@ -87,8 +90,9 @@
     gram_z,
     gram,
     load_sem,
-    prior_send,
-    prior_recv,
+    pair_sems,
+    node_sems,
+    root_sems,
     z_send,
     z_recv,
     p_send,
@@ -128,9 +132,7 @@
     def tile_of(owner):
         return pl.ds(pl.multiple_of(owner * LANES, LANES), LANES)
 
-    own_prior = pltpu.make_async_copy(
-        prior_hbm.at[:, tile_of(me)], prior.at[me], load_sem.at[2 + 2 * n_tp]
-    )
+    own_prior = pltpu.make_async_copy(prior_hbm, prior, load_sem.at[2 + 2 * n_tp])
     own_prior.start()
 
     barrier = pltpu.get_barrier_semaphore()
@@ -140,19 +142,29 @@
         pl.semaphore_signal(barrier, inc=1, device_id={"tensor": tp_of(k)}, device_id_type=MESH)
     pl.semaphore_wait(barrier, n_dp + n_tp - 2)
 
-    prior_copies = []
-    for k in range(1, n_dp):
-        prior_copies.append(
-            pltpu.make_async_remote_copy(
-                src_ref=prior_hbm.at[:, tile_of(dp_of(k))],
-                dst_ref=prior.at[me],
-                send_sem=prior_send.at[k],
-                recv_sem=prior_recv.at[k],
-                device_id={"dp": dp_of(k)},
-                device_id_type=MESH,
-            )
+    half = n_dp // 2
+    core, chip = lax.rem(me, 2), me // 2
+    partner = me + 1 - 2 * core
+    chip_x = chip + 1 - 2 * lax.rem(chip, 2)
+    chip_y = chip + 2 - 4 * (chip // 2)
+    chip_d = half - 1 - chip
+
+    def push(source, target, device, sems, index):
+        copy = pltpu.make_async_remote_copy(
+            src_ref=source,
+            dst_ref=target,
+            send_sem=sems.at[0, index],
+            recv_sem=sems.at[1, index],
+            device_id={"dp": device},
+            device_id_type=MESH,
         )
-        prior_copies[-1].start()
+        copy.start()
+        return copy
+
+    pair_copies = [
+        push(prior_hbm.at[:, tile_of(2 * q + 1 - core)], pair_in.at[q], partner, pair_sems, q)
+        for q in range(half)
+    ]
 
     def exchange(axis, phase, source, target):
         size, other = (n_tp, tp_of) if axis == "tensor" else (n_dp, dp_of)
@@ -195,6 +207,24 @@
             )
             copy.start()
             side_copies.append(copy)
+
+    first_mix, second_mix = mix_ref[:, :rows], mix_ref[:, rows:]
+    own_prior.wait()
+    for copy in pair_copies:
+        copy.wait()
+    own_first = order_ref[2 * chip] == core
+    own_half = [prior[:, tile_of(2 * q + core)] for q in range(half)]
+    firsts = [jnp.where(own_first, own_half[q], pair_in[q]) for q in range(half)]
+    seconds = [jnp.where(own_first, pair_in[q], own_half[q]) for q in range(half)]
+    mixed = dot_high(first_mix, jnp.concatenate(firsts, axis=1))
+    mixed = mixed + dot_high(second_mix, jnp.concatenate(seconds, axis=1))
+    for q in range(half):
+        node_send[q] = mixed[:, q * LANES : (q + 1) * LANES]
+    node_copies = [
+        push(node_send.at[other], node_recv.at[chip], 2 * other + core, node_sems, index)
+        for index, other in enumerate((chip_x, chip_y, chip_d))
+    ]
+    node_recv[chip] = node_send[chip]
     for copy in side_copies:
         copy.wait()
     sides = zrecv[0]
@@ -212,7 +242,44 @@
     for index in range(n_tp):
         zsend[n_tp + index, 0:n_dp, :] = mine[index * n_dp : (index + 1) * n_dp]
     grads[z] = zsend[n_tp + z, 0:n_dp, :]
-    for copy in exchange("tensor", 1, lambda t: zsend.at[n_tp + t, 0:n_dp, :], grads.at[z]):
+    grad_copies = exchange("tensor", 1, lambda t: zsend.at[n_tp + t, 0:n_dp, :], grads.at[z])
+
+    for copy in node_copies:
+        copy.wait()
+    flags = [
+        [order_ref[j * 2 ** (level + 1) + 2**level - 1] == 1 for j in range(n_dp >> (level + 1))]
+        for level in range(levels)
+    ]
+
+    def pick(flip, lower, upper):
+        first = [jnp.where(flip, b, a) for a, b in zip(lower, upper)]
+        return first, [jnp.where(flip, a, b) for a, b in zip(lower, upper)]
+
+    fold_rows = fold_ref[...]
+    paths = [[jnp.concatenate([dot_rows(fold_rows, first_mix), dot_rows(fold_rows, second_mix)], axis=0)]]
+    for level in range(1, levels):
+        paths.append(
+            [dot_rows(p, first_mix) for p in paths[-1]] + [dot_rows(p, second_mix) for p in paths[-1]]
+        )
+    paths = [[p.T for p in level_paths] for level_paths in paths]
+    mixtures = [[[node_recv[j]] for j in range(half)]]
+    for level in range(1, levels):
+        below = mixtures[-1]
+        sides_of = [pick(flags[level][j], below[2 * j], below[2 * j + 1]) for j in range(len(below) // 2)]
+        count = len(below[0])
+        left = dot_high(first_mix, jnp.concatenate([v for first, _ in sides_of for v in first], axis=1))
+        right = dot_high(second_mix, jnp.concatenate([v for _, second in sides_of for v in second], axis=1))
+        mixtures.append(
+            [
+                [
+                    side[:, (j * count + i) * LANES : (j * count + i + 1) * LANES]
+                    for side in (left, right)
+                    for i in range(count)
+                ]
+                for j in range(len(sides_of))
+            ]
+        )
+    for copy in grad_copies:
         copy.wait()
     for index in range(n_tp):
         value = grads[index]
@@ -220,51 +287,49 @@
             grads_by_tile[tile, index : index + 1, :] = value[tile : tile + 1]
     grads_all[me] = grads_by_tile[me]
     grad_copies = exchange("dp", 0, lambda t: grads_by_tile.at[t], grads_all.at[me])
-    own_prior.wait()
-    for copy in prior_copies:
-        copy.wait()
-    for copy in grad_copies:
-        copy.wait()
-
-    fold = fold_ref[...].T
-    sums = []
-
-    def total(value):
-        sums.append(jnp.sum(jnp.sum(value, axis=0, keepdims=True), axis=1, keepdims=True))
-        return len(sums) - 1
-
-    leaves, leaf_mass = [], []
-    for r in range(n_dp):
-        leaf = prior[r]
-        step = grads_all[r]
+    fold = fold_rows.T
+    leaf_square = jnp.zeros((rows, LANES), f32)
+    for tile in range(n_dp):
+        leaf = prior[:, tile * LANES : (tile + 1) * LANES]
+        step = grads_by_tile[tile]
         for e in range(n_tp):
             leaf = leaf + fold[:, e : e + 1] * step[e : e + 1, :]
-        leaf_mass.append(total(leaf * leaf))
-        leaves.append([leaf])
-    first_mix, second_mix = mix_ref[:, :rows], mix_ref[:, rows:]
-    nodes, products, flags = leaves, [], []
+        leaf_square = leaf_square + leaf * leaf
+
+    def total(value):
+        return jnp.sum(jnp.sum(value, axis=0, keepdims=True), axis=1, keepdims=True)
+
+    own_mass = total(leaf_square)
+    for copy in grad_copies:
+        copy.wait()
+
+    sums, products, nodes = [], [], []
+    steps_of = [[grads_all[r]] for r in range(n_dp)]
     for level in range(levels):
-        merged, level_products, level_flags = [], [], []
-        for j in range(len(nodes) // 2):
-            flip = order_ref[j * 2 ** (level + 1) + 2**level - 1] == 1
-            level_flags.append(flip)
-            lower, upper = nodes[2 * j], nodes[2 * j + 1]
-            first = [jnp.where(flip, b, a) for a, b in zip(lower, upper)]
-            second = [jnp.where(flip, a, b) for a, b in zip(lower, upper)]
-            parts = [dot_high(first_mix, a) for a in first] + [dot_high(second_mix, a) for a in second]
+        level_products, level_nodes, merged_steps = [], [], []
+        for j in range(len(steps_of) // 2):
+            first, second = pick(flags[level][j], steps_of[2 * j], steps_of[2 * j + 1])
             if level == 0:
-                parts = [parts[0] + parts[1]]
-            merged.append(parts)
-            level_products.append(
-                {(a, b): total(parts[a] * parts[b]) for a in range(len(parts)) for b in range(a + 1)}
-            )
-        nodes = merged
+                merged_steps.append([jnp.concatenate([first[0], second[0]], axis=0)])
+            else:
+                merged_steps.append(first + second)
+            parts = [
+                v + dot_high(p, g) for v, p, g in zip(mixtures[level][j], paths[level], merged_steps[-1])
+            ]
+            index_of = {}
+            for a in range(len(parts)):
+                for b in range(a + 1):
+                    index_of[a, b] = n_dp + len(sums)
+                    sums.append(total(parts[a] * parts[b]))
+            level_products.append(index_of)
+            level_nodes.append(parts)
+        steps_of = merged_steps
         products.append(level_products)
-        flags.append(level_flags)
+        nodes = level_nodes
     lane = lax.broadcasted_iota(jnp.int32, (8, LANES), 1)
-    packed = jnp.zeros((8, LANES), f32)
+    packed = jnp.where(lane == me, own_mass, jnp.zeros((8, LANES), f32))
     for index, value in enumerate(sums):
-        packed = jnp.where(lane == index, value, packed)
+        packed = jnp.where(lane == n_dp + index, value, packed)
     sums_z[z] = packed
     for copy in exchange("tensor", 2, lambda t: sums_z.at[z], sums_z.at[z]):
         copy.wait()
@@ -283,7 +348,7 @@
     def summed(index):
         return jnp.sum(jnp.where(lane == index, packed, 0.0), axis=1, keepdims=True)
 
-    masses = [summed(index) for index in leaf_mass]
+    masses = [summed(index) for index in range(n_dp)]
     scales = [[jnp.ones((1, 1), f32)] for _ in range(n_dp)]
     for level in range(levels):
         new_masses, new_scales = [], []
@@ -318,7 +383,14 @@
         gram_part[r, block:, :] = jnp.concatenate([targets[r * n_tp : (r + 1) * n_tp], filler], axis=0)
     gram_rs[me] = gram_part[me]
     gram_copies = exchange("dp", 2, lambda t: gram_part.at[t], gram_rs.at[me])
-    root_copies = exchange("dp", 3, lambda t: root.at[:, tile_of(me)], root.at[:, tile_of(me)])
+    dev_x, dev_y, dev_d = (2 * other + core for other in (chip_x, chip_y, chip_d))
+    upper, lower = pl.ds(0, rows // 2), pl.ds(rows // 2, rows // 2)
+
+    def relay(index, owner, device, span=slice(None)):
+        block_of = root.at[span, tile_of(owner)]
+        return push(block_of, block_of, device, root_sems, index)
+
+    relays = [relay(0, me, dev_x), relay(1, me, dev_y), relay(2, me, partner)]
     for index in range(n_tp):
         value = grads[index]
         for tile in range(n_dp):
@@ -329,7 +401,14 @@
     for index in range(1, n_dp):
         part = part + gram_rs[index]
     gram_z[z] = part
-    for copy in exchange("tensor", 3, lambda t: gram_z.at[z], gram_z.at[z]):
+    z_copies = exchange("tensor", 3, lambda t: gram_z.at[z], gram_z.at[z])
+    relays[0].wait_recv()
+    relays.append(relay(3, dev_x, dev_y, upper))
+    relays.append(relay(4, dev_x, partner))
+    relays[1].wait_recv()
+    relays.append(relay(5, dev_y, dev_x, lower))
+    relays.append(relay(6, dev_y, partner))
+    for copy in z_copies:
         copy.wait()
     part = gram_z[0]
     for index in range(1, n_tp):
@@ -338,8 +417,13 @@
     gram[own_rows, :] = part[0:block]
     gram_copies = exchange("dp", 4, lambda t: gram.at[own_rows], gram.at[own_rows])
     rhs_out[...] = part[block : block + n_tp]
-    for copy in root_copies:
-        copy.wait()
+    relays[3].wait_recv()
+    relays[5].wait_recv()
+    relays.append(relay(7, dev_d, partner))
+    for index, copy in enumerate(relays):
+        copy.wait_send()
+        if index not in (0, 1, 3, 5):
+            copy.wait_recv()
     root_write = pltpu.make_async_copy(root, root_out, out_sem.at[0])
     root_write.start()
     for copy in gram_copies:
@@ -415,7 +499,10 @@
             pltpu.VMEM((slots, SEQ, hidden), bf16),
             pltpu.VMEM((RANK, width), bf16),
             pltpu.VMEM((RANK, hidden), bf16),
-            pltpu.VMEM((n_dp, rows, LANES), f32),
+            pltpu.VMEM((rows, columns), f32),
+            pltpu.VMEM((n_dp // 2, rows, LANES), f32),
+            pltpu.VMEM((n_dp // 2, rows, LANES), f32),
+            pltpu.VMEM((n_dp // 2, rows, LANES), f32),
             pltpu.VMEM((2 * n_tp, SEQ, LANES), f32),
             pltpu.VMEM((n_tp, SEQ, LANES), f32),
             pltpu.VMEM((RANK, LANES), f32),
@@ -430,8 +517,9 @@
             pltpu.VMEM((n_tp, part_rows, rows), f32),
             pltpu.VMEM((rows, rows), f32),
             pltpu.SemaphoreType.DMA((3 + 2 * n_tp,)),
-            pltpu.SemaphoreType.DMA((n_dp,)),
-            pltpu.SemaphoreType.DMA((n_dp,)),
+            pltpu.SemaphoreType.DMA((2, n_dp // 2)),
+            pltpu.SemaphoreType.DMA((2, 3)),
+            pltpu.SemaphoreType.DMA((2, 8)),
             pltpu.SemaphoreType.DMA((phases, n_tp)),
             pltpu.SemaphoreType.DMA((phases, n_tp)),
             pltpu.SemaphoreType.DMA((phases, n_dp)),
@@ -538,8 +626,7 @@
         columns == n_dp * LANES
         and slots == n_tp
         and 2 * RANK == LANES
-        and n_dp == 2 ** (n_dp.bit_length() - 1)
-        and n_dp % 8 == 0
+        and n_dp == 8
         and rows % (8 * n_dp) == 0
     )
 

time: 64.8 us -> 63.7 us (0.983)
  Pallas kernels: 63.3 us -> 62.3 us
    pallas_call x1, Pallas kernels: 55.3 us -> 54.2 us  [fused_body(): pl.pallas_call(functools.partial(fused_kernel, n_dp, n_tp), out_shape=(ja...]
where the time goes in v3:
time: 63.7 us; the launch traced here: 63.6 us
  Pallas kernels  62.3 us (98%)
  between operations  1.29 us (2%)
    pallas_call x1, Pallas kernels, fused_body(): pl.pallas_call(functools.partial(fused_kernel, n_dp, n_tp), out_shape=(ja...  54.2 us
    pallas_call x1, Pallas kernels, fused_body(): pl.pallas_call(solve_kernel, out_shape=(jax.ShapeDtypeStruct((rows, colum...  8.04 us

profile of v3, /device:TPU:0, one launch (start us, length us, event | category | flops | bytes accessed | tf_op | source)
XLA Modules:
  0.0 63.6 jit_solution(18446199663817160300)
XLA Ops:
  1.3 54.2 %shard_map.104 = (f32[256,1024]{1,0:T(8,128)}, f32[256,256]{1,0:T(8,128)}, f32[4,256]{1,0:T(4,128)}, f32[4,1024]{1,0:T(4,128)}) custom-call(bf16[512,2048]{1,0:T(8,128)(2,1)} %act_hbm.1, bf16[512,7168]{1,0:T(8,128)(2,1)} %out_hbm.1, bf16[64,2048]{1,0:T(8,128)(2,1)} %bitcast.4, bf16[64,7168]{1,0:T(8,128)(2,1)} %bitcast.3, s32[1]{0:T(128)S(6)} %copy.11.count_ref, ...), custom_call_target="tpu_custom_call" | custom-call | tf_op jit(solution)/shard_map/pallas_call | solution.py:487
  55.5 8.0 %shard_map.105 = (f32[256,1024]{1,0:T(8,128)}, f32[4,1024]{1,0:T(4,128)}) custom-call(f32[256,1024]{1,0:T(8,128)} %get-tuple-element.6.root_hbm, f32[256,256]{1,0:T(8,128)} %get-tuple-element.7.gram_ref, f32[4,256]{1,0:T(4,128)} %get-tuple-element.8.rhs_ref, f32[4,1024]{1,0:T(4,128)} %get-tuple-element.9.grads_ref), custom_call_target="tpu_custom_call" | custom-call | tf_op jit(solution)/shard_map/pallas_call | solution.py:543

commit v4 on v3

--- a/solution.py
+++ b/solution.py
@@ -50,6 +50,16 @@
     out = jnp.dot(a, c, preferred_element_type=jnp.float32)
     out = out + jnp.dot(a, d, preferred_element_type=jnp.float32)
     return out + jnp.dot(b, c, preferred_element_type=jnp.float32)
+
+
+def dot_mid(left, right):
+    return dot_halves(halves(left), halves(right))
+
+
+def stacked(value, order):
+    high = value.astype(jnp.bfloat16).astype(jnp.float32)
+    both = (high, value - high)
+    return jnp.concatenate([both[i] for i in order], axis=0)
 
 
 def fused_kernel(
@@ -216,8 +226,9 @@
     own_half = [prior[:, tile_of(2 * q + core)] for q in range(half)]
     firsts = [jnp.where(own_first, own_half[q], pair_in[q]) for q in range(half)]
     seconds = [jnp.where(own_first, pair_in[q], own_half[q]) for q in range(half)]
-    mixed = dot_high(first_mix, jnp.concatenate(firsts, axis=1))
-    mixed = mixed + dot_high(second_mix, jnp.concatenate(seconds, axis=1))
+    first_halves, second_halves = halves(first_mix), halves(second_mix)
+    mixed = dot_halves(first_halves, halves(jnp.concatenate(firsts, axis=1)))
+    mixed = mixed + dot_halves(second_halves, halves(jnp.concatenate(seconds, axis=1)))
     for q in range(half):
         node_send[q] = mixed[:, q * LANES : (q + 1) * LANES]
     node_copies = [
@@ -232,7 +243,7 @@
         sides = sides + zrecv[index]
     lane = lax.broadcasted_iota(jnp.int32, sides.shape, 1)
     doubled = jnp.where(lane < RANK, sides, pltpu.roll(sides, RANK, 1))
-    product = dot_high(sides.T, doubled) / jnp.sqrt(f32(SEQ))
+    product = dot_mid(sides.T, doubled) / jnp.sqrt(f32(SEQ))
     product = jnp.where(z < count_ref[0], product, jnp.zeros_like(product))
     full[...] = product[RANK:]
     even = full[pl.ds(0, RANK // 2, stride=2), :]
@@ -244,8 +255,6 @@
     grads[z] = zsend[n_tp + z, 0:n_dp, :]
     grad_copies = exchange("tensor", 1, lambda t: zsend.at[n_tp + t, 0:n_dp, :], grads.at[z])
 
-    for copy in node_copies:
-        copy.wait()
     flags = [
         [order_ref[j * 2 ** (level + 1) + 2**level - 1] == 1 for j in range(n_dp >> (level + 1))]
         for level in range(levels)
@@ -261,24 +270,7 @@
         paths.append(
             [dot_rows(p, first_mix) for p in paths[-1]] + [dot_rows(p, second_mix) for p in paths[-1]]
         )
-    paths = [[p.T for p in level_paths] for level_paths in paths]
-    mixtures = [[[node_recv[j]] for j in range(half)]]
-    for level in range(1, levels):
-        below = mixtures[-1]
-        sides_of = [pick(flags[level][j], below[2 * j], below[2 * j + 1]) for j in range(len(below) // 2)]
-        count = len(below[0])
-        left = dot_high(first_mix, jnp.concatenate([v for first, _ in sides_of for v in first], axis=1))
-        right = dot_high(second_mix, jnp.concatenate([v for _, second in sides_of for v in second], axis=1))
-        mixtures.append(
-            [
-                [
-                    side[:, (j * count + i) * LANES : (j * count + i + 1) * LANES]
-                    for side in (left, right)
-                    for i in range(count)
-                ]
-                for j in range(len(sides_of))
-            ]
-        )
+    paths = [[stacked(p, (0, 0, 1)).T.astype(jnp.bfloat16) for p in level] for level in paths]
     for copy in grad_copies:
         copy.wait()
     for index in range(n_tp):
@@ -300,6 +292,26 @@
         return jnp.sum(jnp.sum(value, axis=0, keepdims=True), axis=1, keepdims=True)
 
     own_mass = total(leaf_square)
+
+    for copy in node_copies:
+        copy.wait()
+    mixtures = [[[node_recv[j]] for j in range(half)]]
+    for level in range(1, levels):
+        below = mixtures[-1]
+        sides_of = [pick(flags[level][j], below[2 * j], below[2 * j + 1]) for j in range(len(below) // 2)]
+        count = len(below[0])
+        left = dot_halves(first_halves, halves(jnp.concatenate([v for f, _ in sides_of for v in f], axis=1)))
+        right = dot_halves(second_halves, halves(jnp.concatenate([v for _, g in sides_of for v in g], axis=1)))
+        mixtures.append(
+            [
+                [
+                    side[:, (j * count + i) * LANES : (j * count + i + 1) * LANES]
+                    for side in (left, right)
+                    for i in range(count)
+                ]
+                for j in range(len(sides_of))
+            ]
+        )
     for copy in grad_copies:
         copy.wait()
 
@@ -313,8 +325,18 @@
                 merged_steps.append([jnp.concatenate([first[0], second[0]], axis=0)])
             else:
                 merged_steps.append(first + second)
+        updates = [
+            jnp.dot(
+                path,
+                jnp.concatenate([stacked(g[i], (0, 1, 0)) for g in merged_steps], axis=1).astype(jnp.bfloat16),
+                preferred_element_type=f32,
+            )
+            for i, path in enumerate(paths[level])
+        ]
+        for j in range(len(merged_steps)):
             parts = [
-                v + dot_high(p, g) for v, p, g in zip(mixtures[level][j], paths[level], merged_steps[-1])
+                v + update[:, j * LANES : (j + 1) * LANES]
+                for v, update in zip(mixtures[level][j], updates)
             ]
             index_of = {}
             for a in range(len(parts)):
@@ -374,7 +396,9 @@
         chunk = chunk + c * part
     root[:, tile_of(me)] = chunk
 
-    square = dot_rows(chunk, chunk)
+    square_halves = halves(chunk)
+    square = dot_flip(square_halves[0], square_halves[0]) + dot_flip(*square_halves)
+    square = square + dot_flip(square_halves[1], square_halves[0])
     every = jnp.concatenate([grads_all[r] for r in range(n_dp)], axis=0)
     targets = dot_rows(every, chunk)
     filler = jnp.zeros((part_rows - block - n_tp, rows), f32)

time: 63.7 us -> 56.2 us (0.88)
  Pallas kernels: 62.3 us -> 54.8 us
    pallas_call x1, Pallas kernels: 54.2 us -> 46.7 us  [fused_body(): pl.pallas_call(functools.partial(fused_kernel, n_dp, n_tp), out_shape=(ja...]
where the time goes in v4:
time: 56.2 us; the launch traced here: 56 us
  Pallas kernels  54.8 us (98%)
  between operations  1.29 us (2%)
    pallas_call x1, Pallas kernels, fused_body(): pl.pallas_call(functools.partial(fused_kernel, n_dp, n_tp), out_shape=(ja...  46.7 us
    pallas_call x1, Pallas kernels, fused_body(): pl.pallas_call(solve_kernel, out_shape=(jax.ShapeDtypeStruct((rows, colum...  8.04 us

profile of v4, /device:TPU:0, one launch (start us, length us, event | category | flops | bytes accessed | tf_op | source)
XLA Modules:
  0.0 56.0 jit_solution(957428673760503259)
XLA Ops:
  1.3 46.7 %shard_map.104 = (f32[256,1024]{1,0:T(8,128)}, f32[256,256]{1,0:T(8,128)}, f32[4,256]{1,0:T(4,128)}, f32[4,1024]{1,0:T(4,128)}) custom-call(bf16[512,2048]{1,0:T(8,128)(2,1)} %act_hbm.1, bf16[512,7168]{1,0:T(8,128)(2,1)} %out_hbm.1, bf16[64,2048]{1,0:T(8,128)(2,1)} %bitcast.4, bf16[64,7168]{1,0:T(8,128)(2,1)} %bitcast.3, s32[1]{0:T(128)S(6)} %copy.11.count_ref, ...), custom_call_target="tpu_custom_call" | custom-call | tf_op jit(solution)/shard_map/pallas_call | solution.py:511
  48.0 8.0 %shard_map.105 = (f32[256,1024]{1,0:T(8,128)}, f32[4,1024]{1,0:T(4,128)}) custom-call(f32[256,1024]{1,0:T(8,128)} %get-tuple-element.6.root_hbm, f32[256,256]{1,0:T(8,128)} %get-tuple-element.7.gram_ref, f32[4,256]{1,0:T(4,128)} %get-tuple-element.8.rhs_ref, f32[4,1024]{1,0:T(4,128)} %get-tuple-element.9.grads_ref), custom_call_target="tpu_custom_call" | custom-call | tf_op jit(solution)/shard_map/pallas_call | solution.py:567

commit v5 on v4

--- a/solution.py
+++ b/solution.py
@@ -400,7 +400,9 @@
     square = dot_flip(square_halves[0], square_halves[0]) + dot_flip(*square_halves)
     square = square + dot_flip(square_halves[1], square_halves[0])
     every = jnp.concatenate([grads_all[r] for r in range(n_dp)], axis=0)
-    targets = dot_rows(every, chunk)
+    every_halves = halves(every)
+    targets = dot_flip(every_halves[0], square_halves[0]) + dot_flip(every_halves[0], square_halves[1])
+    targets = targets + dot_flip(every_halves[1], square_halves[0])
     filler = jnp.zeros((part_rows - block - n_tp, rows), f32)
     for r in range(n_dp):
         gram_part[r, 0:block, :] = square[r * block : (r + 1) * block]
@@ -480,10 +482,11 @@
     write = pltpu.make_async_copy(root, root_out, sems.at[1])
     write.start()
     target = rhs_ref[...] * unit
-    solved = dot_rows(target, inverse)
+    inverse_halves = halves(inverse)
+    solved = dot_halves(halves(target), inverse_halves)
     for _ in range(2):
-        solved = solved + dot_rows(target - dot_rows(solved, system), inverse)
-    pre_out[...] = grads_ref[...] - dot_high(solved, root[...])
+        solved = solved + dot_halves(halves(target - dot_high(solved, system)), inverse_halves)
+    pre_out[...] = grads_ref[...] - dot_mid(solved, root[...])
     write.wait()
 
 

time: 56.2 us -> 54.7 us (0.973)
  Pallas kernels: 54.8 us -> 53.2 us
    pallas_call x1, Pallas kernels: 8.04 us -> 6.51 us  [fused_body(): pl.pallas_call(solve_kernel, out_shape=(jax.ShapeDtypeStruct((rows, colum...]
where the time goes in v5:
time: 54.7 us; the launch traced here: 54.5 us
  Pallas kernels  53.2 us (97%)
  between operations  1.29 us (2%)
    pallas_call x1, Pallas kernels, fused_body(): pl.pallas_call(functools.partial(fused_kernel, n_dp, n_tp), out_shape=(ja...  46.7 us
    pallas_call x1, Pallas kernels, fused_body(): pl.pallas_call(solve_kernel, out_shape=(jax.ShapeDtypeStruct((rows, colum...  6.51 us

profile of v5, /device:TPU:0, one launch (start us, length us, event | category | flops | bytes accessed | tf_op | source)
XLA Modules:
  0.0 54.5 jit_solution(9177496844120128206)
XLA Ops:
  1.3 46.7 %shard_map.104 = (f32[256,1024]{1,0:T(8,128)}, f32[256,256]{1,0:T(8,128)}, f32[4,256]{1,0:T(4,128)}, f32[4,1024]{1,0:T(4,128)}) custom-call(bf16[512,2048]{1,0:T(8,128)(2,1)} %act_hbm.1, bf16[512,7168]{1,0:T(8,128)(2,1)} %out_hbm.1, bf16[64,2048]{1,0:T(8,128)(2,1)} %bitcast.4, bf16[64,7168]{1,0:T(8,128)(2,1)} %bitcast.3, s32[1]{0:T(128)S(6)} %copy.11.count_ref, ...), custom_call_target="tpu_custom_call" | custom-call | tf_op jit(solution)/shard_map/pallas_call | solution.py:514
  48.0 6.5 %shard_map.105 = (f32[256,1024]{1,0:T(8,128)}, f32[4,1024]{1,0:T(4,128)}) custom-call(f32[256,1024]{1,0:T(8,128)} %get-tuple-element.6.root_hbm, f32[256,256]{1,0:T(8,128)} %get-tuple-element.7.gram_ref, f32[4,256]{1,0:T(4,128)} %get-tuple-element.8.rhs_ref, f32[4,1024]{1,0:T(4,128)} %get-tuple-element.9.grads_ref), custom_call_target="tpu_custom_call" | custom-call | tf_op jit(solution)/shard_map/pallas_call | solution.py:570
